TPU v7x, 32 devices: a whole 2x2x4 slice. The times are simulated.
32 devices in a mesh: samp: 8 (over z, core), chan: 4 (over y, x).
Axes of the slice: x: 2, y: 2, z: 4, core: 2. Of those that a mesh axis runs over, the one named last changes fastest.
Arguments:
- out_cot: bfloat16 [8, 256, 4096], P('samp', 'chan'), may hold values from -6 to 6
- mix_weight: bfloat16 [256, 256], replicated, may hold values from -0.375 to 0.375
- corr_kernels: float32 [2, 12, 256, 64], P(None, None, 'chan'), may hold values from -0.75 to 0.75
- momentum: int32 [8], P('samp'), may hold values from 0 to 11
- spin_up: int32 [8, 4096], P('samp', 'chan'), may hold values 0 or 1
- layer_input: bfloat16 [8, 256, 4096], P('samp', None, 'chan'), may hold values from -6 to 6
- pre_one: bfloat16 [8, 256, 4096], P('samp', None, 'chan'), may hold values from -6 to 6
- pre_two: bfloat16 [8, 256, 4096], P('samp', None, 'chan'), may hold values from -6 to 6
- conv_weight: bfloat16 [3, 9, 256, 256], replicated, may hold values from -0.125 to 0.125
- dilation: int32 [3, 256], replicated, may hold values from 1 to 4, as said below
Outputs:
- input_grad: bfloat16 [8, 256, 4096], P('samp', None, 'chan')
- weight_grad: float32 [3, 9, 256, 256], P(None, None, 'chan')
Inputs may be any that keep to these rules, and one draw needn't show every extreme that they name: Some channel of every convolution has dilation 4.
All inputs are finite; a program needn't handle non-finite values. No bound on the sum of `spin_up` on one device may be relied on, other than what follows from the above.
Results may differ from a plain program's by a relative error of at most 0.02.
Values may be sent and summed in bfloat16 or wider, within the bound.
A program may use at most 64 MiB of HBM per device.

v0:
```python
import math
import jax
import jax.numpy as jnp
from jax import lax
from jax.sharding import PartitionSpec as P

SIDE = 64
LAYERS = 3
MAXDIL = 4


def with_halo(shard, sides, width):
    for axis, dim in sides:
        size, length = (lax.axis_size(axis), shard.shape[dim])
        up = [(i, (i + 1) % size) for i in range(size)]
        down = [(j, i) for i, j in up]
        last = lax.slice_in_dim(shard, length - width, length, axis=dim)
        leading = lax.slice_in_dim(shard, 0, width, axis=dim)
        before = lax.ppermute(last, axis, up)
        after = lax.ppermute(leading, axis, down)
        shard = jnp.concatenate([before, shard, after], axis=dim)
    return shard


def column_shift(values, step_size, lattice_side, column):
    if step_size == 0:
        return values
    inside = (column - step_size >= 0) & (column - step_size < lattice_side)
    wrapped = step_size - lattice_side if step_size > 0 else step_size + lattice_side
    return jnp.where(inside, jnp.roll(values, step_size, axis=2), jnp.roll(values, wrapped, axis=2))


def on_device(
    out_cot,
    mix_weight,
    corr_kernels,
    momentum,
    spin_up,
    layer_input,
    pre_one,
    pre_two,
    conv_weight,
    dilation,
):
    highest = lax.Precision.HIGHEST
    sample_count = out_cot.shape[0]
    chan_block = out_cot.shape[1]
    site_count = out_cot.shape[2]
    sectors = corr_kernels.shape[1]
    lattice_side = corr_kernels.shape[3]
    slab_cells = layer_input.shape[2]
    own_start = lax.axis_index("chan") * chan_block
    own_rows = lax.dynamic_slice_in_dim(mix_weight, own_start, chan_block, 0)
    input_cot = lax.psum_scatter(
        jnp.einsum("oc,son->csn", own_rows, out_cot, preferred_element_type=jnp.float32),
        "chan",
        scatter_dimension=0,
        tiled=True,
    )
    onehot = (momentum[:, None] == jnp.arange(sectors, dtype=jnp.int32)[None, :]).astype(
        jnp.float32
    )
    picked = jnp.einsum("sk,akci->acsi", onehot, corr_kernels, precision=highest)
    positions = jnp.arange(lattice_side, dtype=jnp.int32)
    circ_table = (
        (positions[None, None, :] - positions[None, :, None]) % lattice_side
        == positions[:, None, None]
    ).astype(jnp.float32)
    circulant = jnp.einsum("acsi,ixy->acsxy", picked, circ_table, precision=highest)
    grid_values = input_cot.reshape(chan_block, sample_count, lattice_side, lattice_side)
    halfway = jnp.einsum("csxX,csxy->csXy", circulant[0], grid_values, precision=highest)
    corr_grad = jnp.einsum("csXy,csyY->scXY", halfway, circulant[1], precision=highest)
    corr_grad = corr_grad.reshape(sample_count, chan_block, site_count).astype(jnp.bfloat16)
    regrouped = lax.all_to_all(corr_grad, "chan", split_axis=2, concat_axis=1, tiled=True)
    spin_gate = jnp.where(spin_up == 1, 1.5, 0.5).astype(jnp.float32)[:, None, :]
    grad_now = (regrouped.astype(jnp.float32) * spin_gate).astype(jnp.bfloat16)
    halo_cells = MAXDIL * SIDE
    column = jnp.arange(slab_cells, dtype=jnp.int32) % lattice_side
    norm_factor = 1.0 / math.sqrt(sample_count * lax.axis_size("samp") * site_count)
    layer_grads = [None] * LAYERS
    input_grad = None
    for conv_level in range(LAYERS - 1, -1, -1):
        slope_base = None
        if conv_level == 0:
            layer_values = layer_input
        else:
            saved_pre = pre_one if conv_level == 1 else pre_two
            slope_base = jnp.tanh(saved_pre.astype(jnp.float32))
            layer_values = slope_base.astype(jnp.bfloat16)
        padded = with_halo(grad_now, (("chan", 2),), halo_cells)
        back_sum = jnp.zeros(grad_now.shape, jnp.float32)
        tap_grads = []
        for row_step in (-1, 0, 1):
            for col_step in (-1, 0, 1):
                tap_index = (row_step + 1) * 3 + col_step + 1
                if row_step == 0 and col_step == 0:
                    combined = grad_now
                else:
                    combined = None
                    for dilate in range(1, MAXDIL + 1):
                        slice_begin = halo_cells - row_step * dilate * lattice_side
                        shifted = column_shift(
                            padded[:, :, slice_begin : slice_begin + slab_cells],
                            col_step * dilate,
                            lattice_side,
                            column,
                        )
                        if combined is None:
                            combined = shifted
                        else:
                            chosen_mask = (dilation[conv_level] == dilate)[None, :, None]
                            combined = jnp.where(chosen_mask, shifted, combined)
                back_sum = back_sum + jnp.einsum(
                    "oc,son->scn",
                    conv_weight[conv_level, tap_index],
                    combined,
                    preferred_element_type=jnp.float32,
                )
                tap_grads.append(
                    jnp.einsum(
                        "son,scn->oc", combined, layer_values, preferred_element_type=jnp.float32
                    )
                    * norm_factor
                )
        local_grad = jnp.stack(tap_grads)
        reduced = lax.psum_scatter(
            local_grad.astype(jnp.bfloat16), "chan", scatter_dimension=1, tiled=True
        )
        layer_grads[conv_level] = lax.psum(reduced, "samp").astype(jnp.float32)
        if conv_level > 0:
            grad_now = (back_sum * (1.0 - slope_base * slope_base)).astype(jnp.bfloat16)
        else:
            input_grad = back_sum.astype(jnp.bfloat16)
    weight_grad = jnp.stack(layer_grads)
    return (input_grad, weight_grad)


def solution(mesh):
    in_specs = (
        P("samp", "chan", None),
        P(),
        P(None, None, "chan", None),
        P("samp"),
        P("samp", "chan"),
        P("samp", None, "chan"),
        P("samp", None, "chan"),
        P("samp", None, "chan"),
        P(),
        P(),
    )
    out_specs = (P("samp", None, "chan"), P(None, None, "chan", None))
    return jax.shard_map(
        on_device, mesh=mesh, in_specs=in_specs, out_specs=out_specs, check_vma=False
    )
```

profile of v0, /device:TPU:0, one launch (start us, length us, event | category | flops | bytes accessed | tf_op | source)
XLA Modules:
  0.0 344.3 jit_solution(6769106226334867354)
XLA Ops:
  7.2 3.8 %convolution_bitcast_fusion = f32[256,1,4096]{2,0,1:T(8,128)} fusion(bf16[1,64,4096]{2,1,0:T(8,128)(2,1)} %param.10, bf16[256,256]{1,0:T(8,128)(2,1)} %param.11, s32[]{:T(128)S(6)} %select_n.3285), kind=kOutput, calls=%fused_computation | convolution fusion | flops 134217728 | bytes 4751364 | tf_op jit(solution)/shard_map/oc,son->csn/dot_general | solution.py:55
  12.7 1.8 fusion.5
  14.5 2.3 slice_bitcast_fusion
  16.8 49.8 %reduce-scatter.5.cloned.1.call-done = f32[64,1,4096]{2,0,1:T(8,128)} async-done(((f32[256,1,4096]{2,0,1:T(8,128)}), f32[64,1,4096]{2,0,1:T(8,128)}) %reduce-scatter.5.cloned.1.call-update) | async-done | bytes 1048592 | tf_op jit(solution)/shard_map/reduce_scatter | solution.py:54
  66.7 2.2 reshape.16731
  68.8 6.2 %fusion.2 = f32[64,64,64]{2,1,0:T(8,128)S(1)} fusion(f32[64,64,64]{2,1,0:T(8,128)S(1)} %reshape.16731, f32[64,64,64]{2,0,1:T(8,128)} %get-tuple-element.25), kind=kOutput, calls=%fused_computation.119 | convolution fusion | flops 201326592 | bytes 3145728 | tf_op jit(solution)/shard_map/csxX,csxy->csXy/dot_general | solution.py:71
  75.0 3.3 fusion.7
  79.2 2.8 copy.42
  82.5 23.6 %reduce.18 = bf16[4096,64]{1,0:T(8,128)(2,1)} reduce(bf16[4096,1,64]{2,1,0:T(2,128)(2,1)S(1)} %bitcast.976, bf16[]{:T(256)} %broadcast.4323), dimensions={1}, to_apply=%bitcast.918.reduce_sub_computation | reduce | bytes 1048578
  106.1 2.7 reshape.16776
  108.7 3.5 %all-to-all-start = ((bf16[4,2,32768]{2,1,0:T(2,128)(2,1)}), bf16[4,2,32768]{2,1,0:T(2,128)(2,1)S(1)}, u32[]{:S(2)}, u32[]{:S(2)}) async-start(bf16[4,2,32768]{2,1,0:T(2,128)(2,1)} %reshape.16776), calls=%async_computation.1 | async-start | bytes 1048576 | tf_op jit(solution)/shard_map/all_to_all | solution.py:74
  114.4 6.1 %all-to-all-done = bf16[4,2,32768]{2,1,0:T(2,128)(2,1)S(1)} async-done(((bf16[4,2,32768]{2,1,0:T(2,128)(2,1)}), bf16[4,2,32768]{2,1,0:T(2,128)(2,1)S(1)}, u32[]{:S(2)}, u32[]{:S(2)}) %all-to-all-start) | async-done | bytes 524320 | tf_op jit(solution)/shard_map/all_to_all | solution.py:74
  121.3 2.3 copy.43
  126.2 1.5 collective-permute-start.1
  127.7 1.9 collective-permute-start
  129.6 4.8 %collective-permute-done = bf16[1,256,256]{1,2,0:T(8,128)(2,1)S(1)} collective-permute-done((bf16[1,256,256]{1,2,0:T(8,128)(2,1)S(1)}, bf16[1,256,256]{1,2,0:T(8,128)(2,1)S(1)}, u32[]{:S(2)}, u32[]{:S(2)}) %collective-permute-start) | collective-permute-done | bytes 131104 | tf_op jit(solution)/shard_map/ppermute | solution.py:20
  137.4 3.0 fusion.252
  143.4 3.0 fusion.256
  147.6 3.0 fusion.260
  151.8 1.3 convolution_add_fusion.20
  153.1 3.0 fusion.264
  157.4 3.0 fusion.268
  162.9 3.0 fusion.272
  165.9 1.2 fusion.14
  168.8 2.0 collective-permute-start.2
  177.7 3.0 fusion.276
  183.7 3.0 fusion.280
  186.7 1.2 convolution_add_fusion.14
  187.9 3.0 fusion.284
  193.4 3.0 fusion.288
  197.6 3.0 fusion.292
  203.1 3.0 fusion.296
  206.2 1.2 fusion.15
  208.5 2.0 collective-permute-start.4
  218.1 3.0 fusion.300
  223.8 3.0 fusion.304
  227.8 3.0 fusion.308
  232.9 3.0 fusion.312
  236.8 3.0 fusion.316
  241.9 3.0 fusion.320
  249.6 1.3 convolution_add_fusion.5
  250.8 1.3 convolution_add_fusion.4
  252.1 1.2 convolution_add_fusion.3
  253.4 1.3 convolution_add_fusion.2
  254.7 20.1 %reduce-scatter.7.cloned.1.call-done = bf16[9,64,256]{2,1,0:T(8,128)(2,1)} async-done(((bf16[9,256,256]{2,1,0:T(8,128)(2,1)}), bf16[9,64,256]{2,1,0:T(8,128)(2,1)}) %reduce-scatter.7.cloned.1.call-update) | async-done | bytes 294928 | tf_op jit(solution)/shard_map/reduce_scatter | solution.py:126
  276.1 1.3 fusion.17
  278.4 56.7 %all-reduce.3.cloned.1.call-done = (bf16[1,9,64,256]{3,2,1,0:T(8,128)(2,1)}, bf16[1,9,64,256]{3,2,1,0:T(8,128)(2,1)}, bf16[1,9,64,256]{3,2,1,0:T(8,128)(2,1)}) async-done(((bf16[1,9,64,256]{3,2,1,0:T(8,128)(2,1)}, bf16[1,9,64,256]{3,2,1,0:T(8,128)(2,1)}, bf16[1,9,64,256]{3,2,1,0:T(8,128)(2,1)}), (bf16[1,9,64,256]{3,2,1,0:T(8,128)(2,1)}, bf16[1,9,64,256]{3,2,1,0:T(8,128)(2,1)}, ...) | async-done | bytes 884752 | tf_op jit(solution)/shard_map/psum | solution.py:129
  335.0 2.5 maximum_convert_fusion
  (226 shorter events, 61.1 us)
Async XLA Ops:
  7.2 4.7 %copy-start = (f32[2,12,64,64]{3,2,1,0:T(8,128)S(1)}, f32[2,12,64,64]{3,2,1,0:T(8,128)}, u32[]{:S(2)}) copy-start(f32[2,12,64,64]{3,2,1,0:T(8,128)} %param.12) | copy-start | bytes 1179652
  7.2 59.5 %reduce-scatter.5.cloned.1.call-start = ((), (), s32[]{:S(2)}) async-start(), calls=%async_computation.5 | async-start | bytes 5242880 | tf_op jit(solution)/shard_map/reduce_scatter | solution.py:54
  68.8 6.2 %copy-start.2 = (f32[64,64,64]{2,0,1:T(8,128)S(1)}, f32[64,64,64]{2,0,1:T(8,128)}, u32[]{:S(2)}) copy-start(f32[64,64,64]{2,0,1:T(8,128)} %get-tuple-element.24) | copy-start | bytes 3145732
  106.1 6.2 %copy-start.15 = (bf16[1,256,1024]{2,1,0:T(8,128)(2,1)S(1)}, bf16[1,256,1024]{2,1,0:T(8,128)(2,1)}, u32[]{:S(2)}) copy-start(bf16[1,256,1024]{2,1,0:T(8,128)(2,1)} %param.16) | copy-start | bytes 1572868
  106.1 7.2 %copy-start.16 = (bf16[1,256,1024]{2,1,0:T(8,128)(2,1)S(1)}, bf16[1,256,1024]{2,1,0:T(8,128)(2,1)}, u32[]{:S(2)}) copy-start(bf16[1,256,1024]{2,1,0:T(8,128)(2,1)} %param.17) | copy-start | bytes 1572868
  106.1 8.2 %copy-start.18 = (s32[3,256]{1,0:T(4,128)S(1)}, s32[3,256]{1,0:T(4,128)}, u32[]{:S(2)}) copy-start(s32[3,256]{1,0:T(4,128)} %param.19) | copy-start | bytes 9220
  106.1 8.3 %copy-start.17 = (s32[1,1024]{1,0:T(1,128)S(1)}, s32[1,1024]{1,0:T(1,128)}, u32[]{:S(2)}) copy-start(s32[1,1024]{1,0:T(1,128)} %param.14) | copy-start | bytes 12292
  108.7 11.7 %all-to-all-start = ((bf16[4,2,32768]{2,1,0:T(2,128)(2,1)}), bf16[4,2,32768]{2,1,0:T(2,128)(2,1)S(1)}, u32[]{:S(2)}, u32[]{:S(2)}) async-start(bf16[4,2,32768]{2,1,0:T(2,128)(2,1)} %reshape.16776), calls=%async_computation.1 | async-start | bytes 1048576 | tf_op jit(solution)/shard_map/all_to_all | solution.py:74
  112.2 142.5 %reduce-scatter.11.cloned.1.call-start = ((), (), s32[]{:S(2)}) async-start(), calls=%async_computation.8 | async-start | bytes 1474560 | tf_op jit(solution)/shard_map/reduce_scatter | solution.py:126
  126.2 8.3 %collective-permute-start.1 = (bf16[1,256,256]{1,2,0:T(8,128)(2,1)S(1)}, bf16[1,256,256]{1,2,0:T(8,128)(2,1)S(1)}, u32[]{:S(2)}, u32[]{:S(2)}) collective-permute-start(bf16[1,256,256]{1,2,0:T(8,128)(2,1)S(1)} %get-tuple-element.324), channel_id=1, source_target_pairs={{0,1},{1,2},{2,3},{3,0},{4,5},{5,6},{6,7},{7,4},{8,9},{9,10},{10,1... | collective-permute-start | bytes 393224 | tf_op jit(solution)/shard_map/ppermute | solution.py:19
  127.7 6.7 %collective-permute-start = (bf16[1,256,256]{1,2,0:T(8,128)(2,1)S(1)}, bf16[1,256,256]{1,2,0:T(8,128)(2,1)S(1)}, u32[]{:S(2)}, u32[]{:S(2)}) collective-permute-start(bf16[1,256,256]{1,2,0:T(8,128)(2,1)S(1)} %get-tuple-element.325), channel_id=1, source_target_pairs={{1,0},{2,1},{3,2},{0,3},{5,4},{6,5},{7,6},{4,7},{9,8},{10,9},{11,1... | collective-permute-start | bytes 393224 | tf_op jit(solution)/shard_map/ppermute | solution.py:20
  162.9 3.0 copy-start.8
  167.7 7.3 %collective-permute-start.3 = (bf16[1,256,256]{1,2,0:T(8,128)(2,1)S(1)}, bf16[1,256,256]{1,2,0:T(8,128)(2,1)S(1)}, u32[]{:S(2)}, u32[]{:S(2)}) collective-permute-start(bf16[1,256,256]{1,2,0:T(8,128)(2,1)S(1)} %get-tuple-element.258), channel_id=1, source_target_pairs={{0,1},{1,2},{2,3},{3,0},{4,5},{5,6},{6,7},{7,4},{8,9},{9,10},{10,1... | collective-permute-start | bytes 393224 | tf_op jit(solution)/shard_map/ppermute | solution.py:19
  168.8 6.1 %collective-permute-start.2 = (bf16[1,256,256]{1,2,0:T(8,128)(2,1)S(1)}, bf16[1,256,256]{1,2,0:T(8,128)(2,1)S(1)}, u32[]{:S(2)}, u32[]{:S(2)}) collective-permute-start(bf16[1,256,256]{1,2,0:T(8,128)(2,1)S(1)} %get-tuple-element.259), channel_id=1, source_target_pairs={{1,0},{2,1},{3,2},{0,3},{5,4},{6,5},{7,6},{4,7},{9,8},{10,9},{11,1... | collective-permute-start | bytes 393224 | tf_op jit(solution)/shard_map/ppermute | solution.py:20
  173.8 1.0 copy-start.13
  174.8 79.9 %reduce-scatter.9.cloned.1.call-start = ((), (), s32[]{:S(2)}) async-start(), calls=%async_computation.7 | async-start | bytes 1474560 | tf_op jit(solution)/shard_map/reduce_scatter | solution.py:126
  203.1 3.0 copy-start.7
  207.6 7.8 %collective-permute-start.5 = (bf16[1,256,256]{1,2,0:T(8,128)(2,1)S(1)}, bf16[1,256,256]{1,2,0:T(8,128)(2,1)S(1)}, u32[]{:S(2)}, u32[]{:S(2)}) collective-permute-start(bf16[1,256,256]{1,2,0:T(8,128)(2,1)S(1)} %get-tuple-element.192), channel_id=1, source_target_pairs={{0,1},{1,2},{2,3},{3,0},{4,5},{5,6},{6,7},{7,4},{8,9},{9,10},{10,1... | collective-permute-start | bytes 393224 | tf_op jit(solution)/shard_map/ppermute | solution.py:19
  208.5 6.8 %collective-permute-start.4 = (bf16[1,256,256]{1,2,0:T(8,128)(2,1)S(1)}, bf16[1,256,256]{1,2,0:T(8,128)(2,1)S(1)}, u32[]{:S(2)}, u32[]{:S(2)}) collective-permute-start(bf16[1,256,256]{1,2,0:T(8,128)(2,1)S(1)} %get-tuple-element.193), channel_id=1, source_target_pairs={{1,0},{2,1},{3,2},{0,3},{5,4},{6,5},{7,6},{4,7},{9,8},{10,9},{11,1... | collective-permute-start | bytes 393224 | tf_op jit(solution)/shard_map/ppermute | solution.py:20
  213.9 1.0 copy-start.14
  215.0 59.8 %reduce-scatter.7.cloned.1.call-start = ((), (), s32[]{:S(2)}) async-start(), calls=%async_computation.6 | async-start | bytes 1474560 | tf_op jit(solution)/shard_map/reduce_scatter | solution.py:126
  218.1 3.0 copy-start.19
  222.7 4.1 %copy-start.11 = (bf16[256,1024]{0,1:T(8,128)(2,1)}, bf16[256,1024]{0,1:T(8,128)(2,1)S(1)}, u32[]{:S(2)}) copy-start(bf16[256,1024]{0,1:T(8,128)(2,1)S(1)} %get-tuple-element.123) | copy-start | bytes 1572868
  222.7 18.2 %copy-start.9 = (bf16[256,1024]{0,1:T(8,128)(2,1)}, bf16[256,1024]{0,1:T(8,128)(2,1)S(1)}, u32[]{:S(2)}) copy-start(bf16[256,1024]{0,1:T(8,128)(2,1)S(1)} %get-tuple-element.122) | copy-start | bytes 1572868
  235.8 4.0 %copy-start.3 = (bf16[256,1024]{0,1:T(8,128)(2,1)}, bf16[256,1024]{0,1:T(8,128)(2,1)S(1)}, u32[]{:S(2)}) copy-start(bf16[256,1024]{0,1:T(8,128)(2,1)S(1)} %fusion.312) | copy-start | bytes 1572868
  239.8 2.0 copy-start.5
  244.8 2.3 copy-start.12
  245.9 89.1 %all-reduce.3.cloned.1.call-start = ((), (), s32[]{:S(2)}) async-start(), calls=%async_computation.9 | async-start | bytes 1769472 | tf_op jit(solution)/shard_map/psum | solution.py:129
  249.6 2.6 copy-start.4
  250.8 2.5 copy-start.6
  253.4 21.5 %copy-start.10 = (bf16[256,1024]{0,1:T(8,128)(2,1)S(1)}, bf16[256,1024]{0,1:T(8,128)(2,1)}, u32[]{:S(2)}) copy-start(bf16[256,1024]{0,1:T(8,128)(2,1)} %copy-done.9) | copy-start | bytes 1572868
  276.1 61.5 %copy-start.1 = (f32[2,12,64,64]{3,2,1,0:T(8,128)S(1)}, f32[2,12,64,64]{3,2,1,0:T(8,128)}, u32[]{:S(2)}) copy-start(f32[2,12,64,64]{3,2,1,0:T(8,128)} %param.12) | copy-start | bytes 1179652
Sparse Core Ops, SparseCore 0:
  11.2 55.3 reduce-scatter.4
  174.9 27.8 reduce-scatter.10
  215.1 28.0 reduce-scatter.8
  246.3 28.5 reduce-scatter.6
  277.4 57.5 all-reduce.2
where the time goes:
time: 348 us; the launch traced here: 344 us
  waiting for transfers between devices  138 us (40%)
  other arithmetic  90.3 us (26%)
  matrix products  64.6 us (19%)
  local copies, waits for them, and re-layouts  22.2 us (6%)
  between operations  16.2 us (5%)
  starting transfers between devices  13.4 us (4%)
    psum x1, waiting for transfers between devices, on_device(): layer_grads[conv_level] = lax.psum(reduced, 'samp').astype(jnp.float32)  56.7 us
    select_n x18, other arithmetic, on_device(): combined = jnp.where(chosen_mask, shifted, combined)  54 us
    reduce_scatter x1, waiting for transfers between devices, on_device(): lax.psum_scatter(jnp.einsum('oc,son->csn', own_rows, out_cot, preferred_e...  49.8 us
    dot_general x27, matrix products, on_device(): jnp.einsum('oc,son->scn', conv_weight[conv_level, tap_index], combined, p...  32.9 us
    unnamed x1, other arithmetic  23.6 us
    reduce_scatter x3, waiting for transfers between devices, on_device(): lax.psum_scatter(local_grad.astype(jnp.bfloat16), 'chan', scatter_dimensi...  20.1 us
    dot_general x27, matrix products, on_device(): jnp.einsum('son,scn->oc', combined, layer_values, preferred_element_type=...  15.7 us
    unnamed x46, local copies, waits for them, and re-layouts  9.22 us
  transfers between devices with their start and end apart: 12, of which 5 were waited for; matrix products, arithmetic and copies ran while one was open for 26% of the time, Pallas kernels for 0%

commit v1 on v0

--- a/solution.py
+++ b/solution.py
@@ -7,6 +7,17 @@
 SIDE = 64
 LAYERS = 3
 MAXDIL = 4
+
+
+def in_blocks(x, dim, peers):
+    before, after = (x.shape[:dim], x.shape[dim + 1 :])
+    return jnp.moveaxis(x.reshape(*before, peers, -1, *after), dim, 0)
+
+
+def laid_out(pieces, dim):
+    shape = list(pieces.shape[1:])
+    shape[dim] *= pieces.shape[0]
+    return jnp.moveaxis(pieces, 0, dim).reshape(shape)
 
 
 def with_halo(shard, sides, width):
@@ -71,7 +82,14 @@
     halfway = jnp.einsum("csxX,csxy->csXy", circulant[0], grid_values, precision=highest)
     corr_grad = jnp.einsum("csXy,csyY->scXY", halfway, circulant[1], precision=highest)
     corr_grad = corr_grad.reshape(sample_count, chan_block, site_count).astype(jnp.bfloat16)
-    regrouped = lax.all_to_all(corr_grad, "chan", split_axis=2, concat_axis=1, tiled=True)
+    peers, here = (lax.axis_size("chan"), lax.axis_index("chan"))
+    pieces = in_blocks(corr_grad, 2, peers)
+    outs = [pieces[here]]
+    for hop in range(1, peers):
+        sent = pieces[here ^ hop]
+        outs.append(lax.ppermute(sent, "chan", [(i_2, i_2 ^ hop) for i_2 in range(peers)]))
+    pieces = jnp.stack(outs)[here ^ jnp.arange(peers)]
+    regrouped = laid_out(pieces, 1)
     spin_gate = jnp.where(spin_up == 1, 1.5, 0.5).astype(jnp.float32)[:, None, :]
     grad_now = (regrouped.astype(jnp.float32) * spin_gate).astype(jnp.bfloat16)
     halo_cells = MAXDIL * SIDE

time: 348 us -> 321 us (0.922)
  other arithmetic: 90.3 us -> 67.3 us
  local copies, waits for them, and re-layouts: 22.2 us -> 13.4 us
  matrix products: 64.6 us -> 70.4 us
    unnamed x1 -> x0, other arithmetic: 23.6 us -> none
    all_to_all x1 -> x0, waiting for transfers between devices: 6.09 us -> none  [on_device(): lax.all_to_all(corr_grad, 'chan', split_axis=2, concat_axis=1, tiled=True)]
    unnamed x46 -> x87, local copies, waits for them, and re-layouts: 9.22 us -> 3.17 us
    dot_general x27, matrix products: 15.7 us -> 21.5 us  [on_device(): jnp.einsum('son,scn->oc', combined, layer_values, preferred_element_type=...]
    ppermute x0 -> x3, waiting for transfers between devices: none -> 4.32 us  [on_device(): lax.ppermute(sent, 'chan', [(i_2, i_2 ^ hop) for i_2 in range(peers)])]
    ppermute x0 -> x3, starting transfers between devices: none -> 3.55 us  [on_device(): lax.ppermute(sent, 'chan', [(i_2, i_2 ^ hop) for i_2 in range(peers)])]
  transfers between devices with their start and end apart: 12 -> 14, of which waited for: 5 -> 7; matrix products, arithmetic and copies ran while one was open for 26% -> 30% of each run, Pallas kernels for 0% -> 0%
where the time goes in v1:
time: 321 us; the launch traced here: 317 us
  waiting for transfers between devices  136 us (42%)
  matrix products  70.4 us (22%)
  other arithmetic  67.3 us (21%)
  between operations  16.4 us (5%)
  local copies, waits for them, and re-layouts  13.4 us (4%)
  starting transfers between devices  13.3 us (4%)
    psum x1, waiting for transfers between devices, on_device(): layer_grads[conv_level] = lax.psum(reduced, 'samp').astype(jnp.float32)  56.6 us
    select_n x18, other arithmetic, on_device(): combined = jnp.where(chosen_mask, shifted, combined)  54.1 us
    reduce_scatter x1, waiting for transfers between devices, on_device(): lax.psum_scatter(jnp.einsum('oc,son->csn', own_rows, out_cot, preferred_e...  49.6 us
    dot_general x27, matrix products, on_device(): jnp.einsum('oc,son->scn', conv_weight[conv_level, tap_index], combined, p...  32.8 us
    dot_general x27, matrix products, on_device(): jnp.einsum('son,scn->oc', combined, layer_values, preferred_element_type=...  21.5 us
    reduce_scatter x3, waiting for transfers between devices, on_device(): lax.psum_scatter(local_grad.astype(jnp.bfloat16), 'chan', scatter_dimensi...  19.8 us
    ppermute x3, starting transfers between devices, with_halo(): after = lax.ppermute(leading, axis, down)  7.48 us
  transfers between devices with their start and end apart: 14, of which 7 were waited for; matrix products, arithmetic and copies ran while one was open for 30% of the time, Pallas kernels for 0%

profile of v1, /device:TPU:0, one launch (start us, length us, event | category | flops | bytes accessed | tf_op | source)
XLA Modules:
  0.0 316.8 jit_solution(588304964411034784)
XLA Ops:
  7.2 3.9 %convolution_bitcast_fusion = f32[256,1,4096]{2,0,1:T(8,128)} fusion(bf16[1,64,4096]{2,1,0:T(8,128)(2,1)} %param.10, bf16[256,256]{1,0:T(8,128)(2,1)} %param.11, s32[]{:T(128)S(6)} %select_n.3307), kind=kOutput, calls=%fused_computation.1 | convolution fusion | flops 134217728 | bytes 4751364 | tf_op jit(solution)/shard_map/oc,son->csn/dot_general | solution.py:66
  12.9 1.8 fusion.5
  14.7 2.3 slice_bitcast_fusion
  17.0 49.6 %reduce-scatter.5.cloned.1.call-done = f32[64,1,4096]{2,0,1:T(8,128)} async-done(((f32[256,1,4096]{2,0,1:T(8,128)}), f32[64,1,4096]{2,0,1:T(8,128)}) %reduce-scatter.5.cloned.1.call-update) | async-done | bytes 1048592 | tf_op jit(solution)/shard_map/reduce_scatter | solution.py:65
  66.7 2.2 reshape.16786
  68.9 6.2 %fusion = f32[64,64,64]{2,1,0:T(8,128)S(1)} fusion(f32[64,64,64]{2,1,0:T(8,128)S(1)} %reshape.16786, f32[64,64,64]{2,0,1:T(8,128)} %get-tuple-element.19), kind=kOutput, calls=%fused_computation.118 | convolution fusion | flops 201326592 | bytes 3145728 | tf_op jit(solution)/shard_map/csxX,csxy->csXy/dot_general | solution.py:82
  75.0 3.3 %fusion.7 = bf16[64,64,64]{2,1,0:T(8,128)(2,1)S(1)} fusion(f32[64,64,64]{2,1,0:T(8,128)S(1)} %fusion, f32[64,64,64]{2,0,1:T(8,128)S(1)} %copy-done.2), kind=kOutput, calls=%fused_computation.125 | convolution fusion | flops 201588736 | bytes 2621440 | tf_op jit(solution)/shard_map/csXy,csyY->scXY/dot_general | solution.py:83
  80.3 1.5 collective-permute-start.2
  81.8 1.4 collective-permute-start
  85.0 2.7 collective-permute-done.2
  87.6 1.6 collective-permute-done
  90.7 1.4 collective-permute-start.4
  92.1 1.9 collective-permute-start.3
  94.0 5.5 %collective-permute-done.3 = bf16[1,256,256]{1,2,0:T(8,128)(2,1)S(1)} collective-permute-done((bf16[1,256,256]{1,2,0:T(8,128)(2,1)S(1)}, bf16[1,256,256]{1,2,0:T(8,128)(2,1)S(1)}, u32[]{:S(2)}, u32[]{:S(2)}) %collective-permute-start.3) | collective-permute-done | bytes 131104 | tf_op jit(solution)/shard_map/ppermute | solution.py:31
  102.5 3.0 fusion.252
  108.5 3.0 fusion.256
  112.8 3.0 fusion.260
  117.0 1.3 convolution_add_fusion.20
  118.2 3.0 fusion.264
  122.5 3.0 fusion.268
  125.5 1.2 convolution_add_fusion.18
  126.7 1.2 convolution_add_fusion.17
  128.0 3.0 fusion.272
  131.0 1.2 fusion.14
  133.9 2.6 collective-permute-start.5
  147.7 3.0 fusion.276
  153.6 3.0 fusion.280
  156.6 1.2 convolution_add_fusion.14
  157.8 3.0 fusion.284
  163.3 3.0 fusion.288
  167.6 3.0 fusion.292
  173.1 3.0 fusion.296
  176.1 1.2 fusion.15
  180.0 2.9 collective-permute-start.7
  190.9 3.0 fusion.300
  196.5 3.0 fusion.304
  200.6 3.0 fusion.308
  205.7 3.0 fusion.312
  209.7 3.0 fusion.316
  214.7 3.0 fusion.320
  222.5 1.3 convolution_add_fusion.5
  223.7 1.3 convolution_add_fusion.4
  225.0 1.2 convolution_add_fusion.3
  226.3 1.3 convolution_add_fusion.2
  227.6 19.8 %reduce-scatter.7.cloned.1.call-done = bf16[9,64,256]{2,1,0:T(8,128)(2,1)} async-done(((bf16[9,256,256]{2,1,0:T(8,128)(2,1)}), bf16[9,64,256]{2,1,0:T(8,128)(2,1)}) %reduce-scatter.7.cloned.1.call-update) | async-done | bytes 294928 | tf_op jit(solution)/shard_map/reduce_scatter | solution.py:144
  248.6 1.3 fusion.17
  250.9 56.6 %all-reduce.3.cloned.1.call-done = (bf16[1,9,64,256]{3,2,1,0:T(8,128)(2,1)}, bf16[1,9,64,256]{3,2,1,0:T(8,128)(2,1)}, bf16[1,9,64,256]{3,2,1,0:T(8,128)(2,1)}) async-done(((bf16[1,9,64,256]{3,2,1,0:T(8,128)(2,1)}, bf16[1,9,64,256]{3,2,1,0:T(8,128)(2,1)}, bf16[1,9,64,256]{3,2,1,0:T(8,128)(2,1)}), (bf16[1,9,64,256]{3,2,1,0:T(8,128)(2,1)}, bf16[1,9,64,256]{3,2,1,0:T(8,128)(2,1)}, ...) | async-done | bytes 884752 | tf_op jit(solution)/shard_map/psum | solution.py:147
  307.5 2.5 maximum_convert_fusion
  (270 shorter events, 63.0 us)
Async XLA Ops:
  7.2 4.8 %copy-start = (f32[2,12,64,64]{3,2,1,0:T(8,128)S(1)}, f32[2,12,64,64]{3,2,1,0:T(8,128)}, u32[]{:S(2)}) copy-start(f32[2,12,64,64]{3,2,1,0:T(8,128)} %param.12) | copy-start | bytes 1179652
  7.2 59.5 %reduce-scatter.5.cloned.1.call-start = ((), (), s32[]{:S(2)}) async-start(), calls=%async_computation.4 | async-start | bytes 5242880 | tf_op jit(solution)/shard_map/reduce_scatter | solution.py:65
  11.1 0.9 copy-start.37
  11.1 216.4 %reduce-scatter.11.cloned.1.call-start = ((), (), s32[]{:S(2)}) async-start(), calls=%async_computation.7 | async-start | bytes 1474560 | tf_op jit(solution)/shard_map/reduce_scatter | solution.py:144
  11.9 155.7 %copy-start.14 = (pred[1024]{0:T(1024)(128)(4,1)}, pred[1024]{0:T(1024)(128)(4,1)S(1)}, u32[]{:S(2)}) copy-start(pred[1024]{0:T(1024)(128)(4,1)S(1)} %get-tuple-element.324) | copy-start | bytes 3076
  11.9 155.7 %copy-start.16 = (pred[1024]{0:T(1024)(128)(4,1)}, pred[1024]{0:T(1024)(128)(4,1)S(1)}, u32[]{:S(2)}) copy-start(pred[1024]{0:T(1024)(128)(4,1)S(1)} %get-tuple-element.325) | copy-start | bytes 3076
  68.8 6.2 %copy-start.2 = (f32[64,64,64]{2,0,1:T(8,128)S(1)}, f32[64,64,64]{2,0,1:T(8,128)}, u32[]{:S(2)}) copy-start(f32[64,64,64]{2,0,1:T(8,128)} %get-tuple-element.18) | copy-start | bytes 3145732
  78.4 5.5 %copy-start.12 = (bf16[1,256,1024]{2,1,0:T(8,128)(2,1)S(1)}, bf16[1,256,1024]{2,1,0:T(8,128)(2,1)}, u32[]{:S(2)}) copy-start(bf16[1,256,1024]{2,1,0:T(8,128)(2,1)} %param.16) | copy-start | bytes 1572868
  79.0 5.1 %copy-start.13 = (bf16[1,256,1024]{2,1,0:T(8,128)(2,1)S(1)}, bf16[1,256,1024]{2,1,0:T(8,128)(2,1)}, u32[]{:S(2)}) copy-start(bf16[1,256,1024]{2,1,0:T(8,128)(2,1)} %param.17) | copy-start | bytes 1572868
  80.1 4.2 %copy-start.38 = (s32[3,256]{1,0:T(4,128)S(1)}, s32[3,256]{1,0:T(4,128)}, u32[]{:S(2)}) copy-start(s32[3,256]{1,0:T(4,128)} %param.19) | copy-start | bytes 9220
  80.3 7.4 %collective-permute-start.2 = (bf16[1,64,1024]{2,1,0:T(8,128)(2,1)S(1)}, bf16[1,64,1024]{2,1,0:T(8,128)(2,1)S(1)}, u32[]{:S(2)}, u32[]{:S(2)}) collective-permute-start(bf16[1,64,1024]{2,1,0:T(8,128)(2,1)S(1)} %bitcast.1005), channel_id=1, source_target_pairs={{0,3},{1,2},{2,1},{3,0},{4,7},{5,6},{6,5},{7,4},{8,11},{9,10},{10,... | collective-permute-start | bytes 393224 | tf_op jit(solution)/shard_map/ppermute | solution.py:90
  81.8 7.4 %collective-permute-start = (bf16[1,64,1024]{2,1,0:T(8,128)(2,1)S(1)}, bf16[1,64,1024]{2,1,0:T(8,128)(2,1)S(1)}, u32[]{:S(2)}, u32[]{:S(2)}) collective-permute-start(bf16[1,64,1024]{2,1,0:T(8,128)(2,1)S(1)} %bitcast.1004), channel_id=1, source_target_pairs={{0,1},{1,0},{2,3},{3,2},{4,5},{5,4},{6,7},{7,6},{8,9},{9,8},{10,11... | collective-permute-start | bytes 393224 | tf_op jit(solution)/shard_map/ppermute | solution.py:90
  83.2 6.1 %collective-permute-start.1 = (bf16[1,64,1024]{2,1,0:T(8,128)(2,1)S(1)}, bf16[1,64,1024]{2,1,0:T(8,128)(2,1)S(1)}, u32[]{:S(2)}, u32[]{:S(2)}) collective-permute-start(bf16[1,64,1024]{2,1,0:T(8,128)(2,1)S(1)} %bitcast.1003), channel_id=1, source_target_pairs={{0,2},{1,3},{2,0},{3,1},{4,6},{5,7},{6,4},{7,5},{8,10},{9,11},{10,... | collective-permute-start | bytes 393224 | tf_op jit(solution)/shard_map/ppermute | solution.py:90
  83.9 89.2 %copy-start.18 = (pred[1024]{0:T(1024)(128)(4,1)}, pred[1024]{0:T(1024)(128)(4,1)S(1)}, u32[]{:S(2)}) copy-start(pred[1024]{0:T(1024)(128)(4,1)S(1)} %get-tuple-element.328) | copy-start | bytes 3076
  83.9 89.2 %copy-start.20 = (pred[1024]{0:T(1024)(128)(4,1)}, pred[1024]{0:T(1024)(128)(4,1)S(1)}, u32[]{:S(2)}) copy-start(pred[1024]{0:T(1024)(128)(4,1)S(1)} %get-tuple-element.329) | copy-start | bytes 3076
  90.7 8.9 %collective-permute-start.4 = (bf16[1,256,256]{1,2,0:T(8,128)(2,1)S(1)}, bf16[1,256,256]{1,2,0:T(8,128)(2,1)S(1)}, u32[]{:S(2)}, u32[]{:S(2)}) collective-permute-start(bf16[1,256,256]{1,2,0:T(8,128)(2,1)S(1)} %get-tuple-element.318), channel_id=1, source_target_pairs={{0,1},{1,2},{2,3},{3,0},{4,5},{5,6},{6,7},{7,4},{8,9},{9,10},{10,1... | collective-permute-start | bytes 393224 | tf_op jit(solution)/shard_map/ppermute | solution.py:30
  92.1 7.4 %collective-permute-start.3 = (bf16[1,256,256]{1,2,0:T(8,128)(2,1)S(1)}, bf16[1,256,256]{1,2,0:T(8,128)(2,1)S(1)}, u32[]{:S(2)}, u32[]{:S(2)}) collective-permute-start(bf16[1,256,256]{1,2,0:T(8,128)(2,1)S(1)} %get-tuple-element.319), channel_id=1, source_target_pairs={{1,0},{2,1},{3,2},{0,3},{5,4},{6,5},{7,6},{4,7},{9,8},{10,9},{11,1... | collective-permute-start | bytes 393224 | tf_op jit(solution)/shard_map/ppermute | solution.py:31
  133.5 11.5 %collective-permute-start.6 = (bf16[1,256,256]{1,2,0:T(8,128)(2,1)S(1)}, bf16[1,256,256]{1,2,0:T(8,128)(2,1)S(1)}, u32[]{:S(2)}, u32[]{:S(2)}) collective-permute-start(bf16[1,256,256]{1,2,0:T(8,128)(2,1)S(1)} %get-tuple-element.252), channel_id=1, source_target_pairs={{0,1},{1,2},{2,3},{3,0},{4,5},{5,6},{6,7},{7,4},{8,9},{9,10},{10,1... | collective-permute-start | bytes 393224 | tf_op jit(solution)/shard_map/ppermute | solution.py:30
  133.9 10.9 %collective-permute-start.5 = (bf16[1,256,256]{1,2,0:T(8,128)(2,1)S(1)}, bf16[1,256,256]{1,2,0:T(8,128)(2,1)S(1)}, u32[]{:S(2)}, u32[]{:S(2)}) collective-permute-start(bf16[1,256,256]{1,2,0:T(8,128)(2,1)S(1)} %get-tuple-element.253), channel_id=1, source_target_pairs={{1,0},{2,1},{3,2},{0,3},{5,4},{6,5},{7,6},{4,7},{9,8},{10,9},{11,1... | collective-permute-start | bytes 393224 | tf_op jit(solution)/shard_map/ppermute | solution.py:31
  144.8 82.8 %reduce-scatter.9.cloned.1.call-start = ((), (), s32[]{:S(2)}) async-start(), calls=%async_computation.6 | async-start | bytes 1474560 | tf_op jit(solution)/shard_map/reduce_scatter | solution.py:144
  180.0 7.7 %collective-permute-start.8 = (bf16[1,256,256]{1,2,0:T(8,128)(2,1)}, bf16[1,256,256]{1,2,0:T(8,128)(2,1)S(1)}, u32[]{:S(2)}, u32[]{:S(2)}) collective-permute-start(bf16[1,256,256]{1,2,0:T(8,128)(2,1)} %get-tuple-element.186), channel_id=1, source_target_pairs={{0,1},{1,2},{2,3},{3,0},{4,5},{5,6},{6,7},{7,4},{8,9},{9,10},{10,1... | collective-permute-start | bytes 393224 | tf_op jit(solution)/shard_map/ppermute | solution.py:30
  180.0 7.6 %collective-permute-start.7 = (bf16[1,256,256]{1,2,0:T(8,128)(2,1)}, bf16[1,256,256]{1,2,0:T(8,128)(2,1)S(1)}, u32[]{:S(2)}, u32[]{:S(2)}) collective-permute-start(bf16[1,256,256]{1,2,0:T(8,128)(2,1)} %get-tuple-element.187), channel_id=1, source_target_pairs={{1,0},{2,1},{3,2},{0,3},{5,4},{6,5},{7,6},{4,7},{9,8},{10,9},{11,1... | collective-permute-start | bytes 393224 | tf_op jit(solution)/shard_map/ppermute | solution.py:31
  186.3 1.0 copy-start.11
  187.3 60.1 %reduce-scatter.7.cloned.1.call-start = ((), (), s32[]{:S(2)}) async-start(), calls=%async_computation.5 | async-start | bytes 1474560 | tf_op jit(solution)/shard_map/reduce_scatter | solution.py:144
  190.2 0.7 copy-start.22
  190.2 0.7 copy-start.31
  190.9 3.0 copy-start.39
  193.9 2.6 copy-start.19
  193.9 2.6 copy-start.21
  195.4 4.1 %copy-start.9 = (bf16[256,1024]{0,1:T(8,128)(2,1)}, bf16[256,1024]{0,1:T(8,128)(2,1)S(1)}, u32[]{:S(2)}) copy-start(bf16[256,1024]{0,1:T(8,128)(2,1)S(1)} %get-tuple-element.117) | copy-start | bytes 1572868
  195.4 18.3 %copy-start.7 = (bf16[256,1024]{0,1:T(8,128)(2,1)}, bf16[256,1024]{0,1:T(8,128)(2,1)S(1)}, u32[]{:S(2)}) copy-start(bf16[256,1024]{0,1:T(8,128)(2,1)S(1)} %get-tuple-element.116) | copy-start | bytes 1572868
  196.5 4.0 %copy-start.29 = (bf16[1,256,1,1,1,1,4]{1,6,5,4,3,2,0:T(4,128)(2,1)S(1)}, bf16[1,256,1,1,1,1,4]{1,6,5,4,3,2,0:T(4,128)(2,1)}, u32[]{:S(2)}) copy-start(bf16[1,256,1,1,1,1,4]{1,6,5,4,3,2,0:T(4,128)(2,1)} %get-tuple-element.164) | copy-start | bytes 6148
  196.5 4.0 %copy-start.30 = (bf16[1,256,1,1,1,1,3]{1,6,5,4,3,2,0:T(4,128)(2,1)S(1)}, bf16[1,256,1,1,1,1,3]{1,6,5,4,3,2,0:T(4,128)(2,1)}, u32[]{:S(2)}) copy-start(bf16[1,256,1,1,1,1,3]{1,6,5,4,3,2,0:T(4,128)(2,1)} %get-tuple-element.152) | copy-start | bytes 4612
  196.5 4.0 %copy-start.35 = (bf16[1,256,1,1,1,1,2]{1,6,5,4,3,2,0:T(2,128)(2,1)S(1)}, bf16[1,256,1,1,1,1,2]{1,6,5,4,3,2,0:T(2,128)(2,1)}, u32[]{:S(2)}) copy-start(bf16[1,256,1,1,1,1,2]{1,6,5,4,3,2,0:T(2,128)(2,1)} %get-tuple-element.140) | copy-start | bytes 3076
  203.6 2.1 copy-start.27
  203.6 2.1 copy-start.28
  203.6 2.1 copy-start.34
  208.7 4.0 %copy-start.3 = (bf16[256,1024]{0,1:T(8,128)(2,1)}, bf16[256,1024]{0,1:T(8,128)(2,1)S(1)}, u32[]{:S(2)}) copy-start(bf16[256,1024]{0,1:T(8,128)(2,1)S(1)} %fusion.312) | copy-start | bytes 1572868
  212.7 2.0 copy-start.5
  212.7 2.0 copy-start.25
  212.7 2.0 copy-start.26
  212.7 2.0 copy-start.33
  217.7 2.3 copy-start.10
  218.8 88.8 %all-reduce.3.cloned.1.call-start = ((), (), s32[]{:S(2)}) async-start(), calls=%async_computation.8 | async-start | bytes 1769472 | tf_op jit(solution)/shard_map/psum | solution.py:147
  222.5 2.6 copy-start.4
  223.7 2.5 copy-start.6
  226.2 21.2 %copy-start.8 = (bf16[256,1024]{0,1:T(8,128)(2,1)S(1)}, bf16[256,1024]{0,1:T(8,128)(2,1)}, u32[]{:S(2)}) copy-start(bf16[256,1024]{0,1:T(8,128)(2,1)} %copy-done.7) | copy-start | bytes 1572868
  248.6 61.4 %copy-start.1 = (f32[2,12,64,64]{3,2,1,0:T(8,128)S(1)}, f32[2,12,64,64]{3,2,1,0:T(8,128)}, u32[]{:S(2)}) copy-start(f32[2,12,64,64]{3,2,1,0:T(8,128)} %param.12) | copy-start | bytes 1179652
  (6 other events, 4.0 us)
Sparse Core Ops, SparseCore 0:
  11.2 55.3 reduce-scatter.4
  144.9 27.6 reduce-scatter.10
  187.4 27.6 reduce-scatter.8
  218.9 28.4 reduce-scatter.6
  250.0 57.5 all-reduce.2
